TPU v7x, 512 devices: a whole 4x8x8 slice. The times are simulated.
512 devices in a mesh: af: 16 (over z, core), gy: 4 (over x), gz: 8 (over y).
Axes of the slice: x: 4, y: 8, z: 8, core: 2. Of those that a mesh axis runs over, the one named last changes fastest.
Arguments:
- slab: bfloat16 [512, 262144], P('af', ('gy', 'gz')), may hold values from -4000 to 4000
- block_owner: int32 [4, 8, 16], P('gy', 'gz'), may hold values from 0 to 15, each once within a row
- basis_init: float32 [512, 128], replicated, may hold values from -0.25 to 0.25
Outputs:
- triangle: float32 [512, 512], replicated
- basis: float32 [512, 128], replicated
- core: bfloat16 [128, 262144], P(None, ('gy', 'gz', 'af'))
Inputs may be any that keep to these rules, and one draw needn't show every extreme that they name: For every gy and gz index, block_owner[gy, gz, :] is a permutation of the 16 af indices.
All inputs are finite; a program needn't handle non-finite values.
Results may differ from a plain program's by a relative error of at most 0.0049.
Values may be sent and summed in bfloat16 or wider, within the bound.
A program may use at most 64 MiB of HBM per device.

v0:
```python
import jax
import jax.numpy as jnp
from jax import lax
from jax.sharding import PartitionSpec as P

ITERS = 2
exact_mode = lax.Precision.HIGHEST


def orthonormal(matrix):
    inner_prod = jnp.dot(matrix.T, matrix, precision=exact_mode)
    factor = jnp.linalg.cholesky(inner_prod)
    return lax.linalg.triangular_solve(
        factor, matrix, left_side=False, lower=True, transpose_a=True
    )


def on_device(slab, block_owner, basis_init):
    fibers = lax.axis_size("af")
    local_rows = slab.shape[0]
    block_cols = slab.shape[1] // fibers
    owners = block_owner.reshape(fibers)
    labels = jnp.arange(fibers, dtype=jnp.int32)
    onehot = (owners[:, None] == labels[None, :]).astype(jnp.int32)
    source = jnp.sum(onehot * labels[:, None], axis=0)
    pieces = slab.reshape(local_rows, fibers, block_cols)
    arranged = jnp.take(pieces, source, axis=1)
    received = lax.all_to_all(arranged, "af", split_axis=1, concat_axis=0, tiled=True)
    columns = received.reshape(local_rows * fibers, block_cols)
    devices_all = fibers * lax.axis_size("gy") * lax.axis_size("gz")
    divisor = block_cols * devices_all
    gram_local = (
        lax.dot_general(
            columns, columns, (((1,), (1,)), ((), ())), preferred_element_type=jnp.float32
        )
        / divisor
    )
    summed = lax.psum(gram_local, ("af", "gy", "gz"))
    triangle = jnp.linalg.cholesky(summed)
    basis = basis_init
    for sweep in range(ITERS):
        half_basis = orthonormal(jnp.dot(triangle.T, basis, precision=exact_mode))
        basis = orthonormal(jnp.dot(triangle, half_basis, precision=exact_mode))
    narrow = basis.astype(jnp.bfloat16)
    core = jnp.dot(narrow.T, columns, preferred_element_type=jnp.float32).astype(jnp.bfloat16)
    return (triangle, basis, core)


def solution(mesh):
    placed = (P("af", ("gy", "gz")), P("gy", "gz", None), P())
    return jax.shard_map(
        on_device,
        mesh=mesh,
        in_specs=placed,
        out_specs=(P(), P(), P(None, ("gy", "gz", "af"))),
        check_vma=False,
    )
```

profile of v0, /device:TPU:23, one launch (start us, length us, event | category | flops | bytes accessed | tf_op | source)
XLA Modules:
  0.0 510.2 jit_solution(9935144710232852774)
XLA Ops:
  7.2 0.0 all-reduce.3.cloned.1.call-start
  7.2 0.6 copy-done.5
  7.9 0.1 select_reduce_fusion.8
  8.0 1.1 copy.39
  9.1 0.6 gather_fusion
  9.7 0.1 select_bitcast_fusion
  9.8 28.0 %all_to_all.15 = bf16[32,16,512]{2,0,1:T(8,128)(2,1)S(1)} all-to-all(bf16[32,16,512]{2,0,1:T(8,128)(2,1)S(1)} %select_bitcast_fusion), channel_id=1, replica_groups=mesh['af'=16,'gy'=4,'gz'=8] {'af'}, dimensions={1} | all-to-all | bytes 1048576 | tf_op jit(solution)/shard_map/all_to_all | solution.py:28
  37.8 1.4 convolution_multiply_fusion
  39.3 273.1 %all-reduce.3.cloned.1.call-done = f32[512,512]{0,1:T(8,128)} async-done(((f32[512,512]{0,1:T(8,128)}), f32[512,512]{0,1:T(8,128)}) %all-reduce.3.cloned.1.call-update) | async-done | bytes 1048592 | tf_op jit(solution)/shard_map/psum | solution.py:38
  312.4 1.6 copy.30
  314.1 0.2 fusion
  314.3 1.0 copy-done.3
  315.3 11.7 %cholesky.120 = f32[128,128]{1,0:T(8,128)S(1)} custom-call(f32[128,128]{1,0:T(8,128)S(1)} %cholesky.382), custom_call_target="Cholesky" | custom-call | tf_op jit(solution)/shard_map/jit(cholesky)/cholesky | solution.py:39
  327.1 9.8 %custom-call.32 = f32[1,128,128]{1,2,0:T(8,128)S(1)} custom-call(f32[1,128,128]{2,1,0:T(8,128)S(1)} %get-tuple-element.26), custom_call_target="InvertDiagBlocksLowerTriangular" | custom-call | tf_op jit(solution)/shard_map/jit(cholesky)/cholesky | solution.py:39
  336.9 0.1 cholesky.251
  337.0 0.3 constant_dynamic-update-slice_fusion.2
  337.3 0.3 convolution_subtract_fusion
  337.7 11.7 %cholesky.244 = f32[128,128]{1,0:T(8,128)S(1)} custom-call(f32[128,128]{1,0:T(8,128)S(1)} %cholesky.386), custom_call_target="Cholesky" | custom-call | tf_op jit(solution)/shard_map/jit(cholesky)/cholesky | solution.py:39
  349.4 10.1 %custom-call.33 = f32[1,128,128]{1,2,0:T(8,128)S(1)} custom-call(f32[1,128,128]{2,1,0:T(8,128)S(1)} %get-tuple-element.23), custom_call_target="InvertDiagBlocksLowerTriangular" | custom-call | tf_op jit(solution)/shard_map/jit(cholesky)/cholesky | solution.py:39
  359.6 0.3 convolution_dynamic-update-slice_fusion
  359.8 0.4 convolution_subtract_fusion.1
  360.2 11.7 %cholesky.265 = f32[128,128]{1,0:T(8,128)S(1)} custom-call(f32[128,128]{1,0:T(8,128)S(1)} %cholesky.391), custom_call_target="Cholesky" | custom-call | tf_op jit(solution)/shard_map/jit(cholesky)/cholesky | solution.py:39
  372.0 0.6 compare_reduce_fusion.5
  372.6 9.8 %custom-call.34 = f32[1,128,128]{1,2,0:T(8,128)S(1)} custom-call(f32[1,128,128]{2,1,0:T(8,128)S(1)} %get-tuple-element.20), custom_call_target="InvertDiagBlocksLowerTriangular" | custom-call | tf_op jit(solution)/shard_map/jit(cholesky)/cholesky | solution.py:39
  382.4 0.2 convolution_dynamic-update-slice_fusion.1
  382.6 0.4 convolution_subtract_fusion.2
  383.0 11.9 %cholesky.282 = f32[128,128]{1,0:T(8,128)S(1)} custom-call(f32[128,128]{1,0:T(8,128)S(1)} %convolution_subtract_fusion.2), custom_call_target="Cholesky" | custom-call | tf_op jit(solution)/shard_map/jit(cholesky)/cholesky | solution.py:39
  394.9 0.7 compare_reduce_fusion.4
  395.7 0.6 compare_reduce_fusion.6
  398.9 0.1 select_select_fusion
  399.1 1.8 fusion.26
  400.9 0.6 fusion.27
  401.5 0.1 copy.31
  401.6 11.7 %cholesky.340 = f32[128,128]{1,0:T(8,128)S(1)} custom-call(f32[128,128]{1,0:T(8,128)S(1)} %fusion.21), custom_call_target="Cholesky" | custom-call | tf_op jit(solution)/shard_map/jit(cholesky)/cholesky | solution.py:12
  413.4 0.6 compare_reduce_fusion.3
  414.0 0.7 fusion.8
  414.7 9.8 %custom-call.38 = f32[1,128,128]{1,2,0:T(8,128)S(1)} custom-call(f32[1,128,128]{2,1,0:T(8,128)S(1)} %fusion.8), custom_call_target="InvertDiagBlocksLowerTriangular" | custom-call | tf_op jit(solution)/shard_map/triangular_solve/custom-call.8 | solution.py:13
  424.5 0.4 convolution_bitcast_fusion.3
  424.9 1.0 fusion.28
  425.9 0.6 fusion.29
  426.5 0.1 copy.32
  426.6 11.9 %cholesky.351 = f32[128,128]{1,0:T(8,128)S(1)} custom-call(f32[128,128]{1,0:T(8,128)S(1)} %fusion.19), custom_call_target="Cholesky" | custom-call | tf_op jit(solution)/shard_map/jit(cholesky)/cholesky | solution.py:12
  438.6 0.6 compare_reduce_fusion.2
  439.2 0.7 fusion.9
  439.9 9.8 %custom-call.39 = f32[1,128,128]{1,2,0:T(8,128)S(1)} custom-call(f32[1,128,128]{2,1,0:T(8,128)S(1)} %fusion.9), custom_call_target="InvertDiagBlocksLowerTriangular" | custom-call | tf_op jit(solution)/shard_map/triangular_solve/custom-call.8 | solution.py:13
  449.7 0.4 convolution_bitcast_fusion.2
  450.1 1.8 fusion.30
  451.9 0.6 fusion.31
  452.5 0.1 copy.33
  452.6 11.7 %cholesky.362 = f32[128,128]{1,0:T(8,128)S(1)} custom-call(f32[128,128]{1,0:T(8,128)S(1)} %fusion.17), custom_call_target="Cholesky" | custom-call | tf_op jit(solution)/shard_map/jit(cholesky)/cholesky | solution.py:12
  464.4 0.6 compare_reduce_fusion.1
  465.0 0.7 fusion.10
  465.7 10.0 %custom-call.40 = f32[1,128,128]{1,2,0:T(8,128)S(1)} custom-call(f32[1,128,128]{2,1,0:T(8,128)S(1)} %fusion.10), custom_call_target="InvertDiagBlocksLowerTriangular" | custom-call | tf_op jit(solution)/shard_map/triangular_solve/custom-call.8 | solution.py:13
  475.7 0.4 convolution_bitcast_fusion.1
  476.1 1.0 fusion.32
  477.1 0.6 fusion.33
  477.7 0.1 copy.34
  477.8 11.7 %cholesky.373 = f32[128,128]{1,0:T(8,128)S(1)} custom-call(f32[128,128]{1,0:T(8,128)S(1)} %fusion.15), custom_call_target="Cholesky" | custom-call | tf_op jit(solution)/shard_map/jit(cholesky)/cholesky | solution.py:12
  489.6 0.6 compare_reduce_fusion
  490.2 0.7 fusion.11
  490.9 9.8 %custom-call.41 = f32[1,128,128]{1,2,0:T(8,128)S(1)} custom-call(f32[1,128,128]{2,1,0:T(8,128)S(1)} %fusion.11), custom_call_target="InvertDiagBlocksLowerTriangular" | custom-call | tf_op jit(solution)/shard_map/triangular_solve/custom-call.8 | solution.py:13
  500.7 0.4 convolution_bitcast_fusion
  501.1 0.9 convolution_convert_fusion
  502.0 0.8 copy.35
  (29 shorter events, 0.4 us)
Async XLA Ops:
  7.2 391.9 %copy-start = (f32[512,128]{1,0:T(8,128)S(1)}, f32[512,128]{1,0:T(8,128)}, u32[]{:S(2)}) copy-start(f32[512,128]{1,0:T(8,128)} %param.8) | copy-start | bytes 786436
  7.2 0.7 copy-start.5
  7.2 305.2 %all-reduce.3.cloned.1.call-start = ((), (), s32[]{:S(2)}) async-start(), calls=%async_computation.1 | async-start | bytes 2097152 | tf_op jit(solution)/shard_map/psum | solution.py:38
  312.4 1.7 copy-start.2
  314.3 1.0 copy-start.3
  315.3 21.7 %copy-start.4 = (f32[512,512]{1,0:T(8,128)S(1)}, f32[512,512]{1,0:T(8,128)}, u32[]{:S(2)}) copy-start(f32[512,512]{1,0:T(8,128)} %copy-done.3) | copy-start | bytes 3145732
  399.1 77.1 %copy-start.1 = (f32[512,512]{1,0:T(8,128)}, f32[512,512]{1,0:T(8,128)S(1)}, u32[]{:S(2)}) copy-start(f32[512,512]{1,0:T(8,128)S(1)} %select_select_fusion) | copy-start | bytes 3145732
Sparse Core Ops, SparseCore 0:
  39.4 272.9 all-reduce.2
where the time goes:
time: 519 us; the launch traced here: 510 us
  waiting for transfers between devices  273 us (53%)
  other arithmetic  171 us (33%)
  blocking collectives  28 us (5%)
  between operations  17.5 us (3%)
  matrix products  13.8 us (3%)
  local copies, waits for them, and re-layouts  6.28 us (1%)
    psum x1, waiting for transfers between devices, on_device(): summed = lax.psum(gram_local, ('af', 'gy', 'gz'))  273 us
    another operation x14, other arithmetic, on_device(): triangle = jnp.linalg.cholesky(summed)  78.9 us
    another operation x12, other arithmetic, orthonormal(): factor = jnp.linalg.cholesky(inner_prod)  49.8 us
    another operation x8, other arithmetic, orthonormal(): lax.linalg.triangular_solve(factor, matrix, left_side=False, lower=True,...  42.1 us
    all_to_all x1, blocking collectives, on_device(): lax.all_to_all(arranged, 'af', split_axis=1, concat_axis=0, tiled=True)  28 us
  transfers between devices with their start and end apart: 1, of which 1 were waited for; matrix products, arithmetic and copies ran while one was open for 0% of the time, Pallas kernels for 0%

commit v1 on v0

--- a/solution.py
+++ b/solution.py
@@ -35,7 +35,9 @@
         )
         / divisor
     )
-    summed = lax.psum(gram_local, ("af", "gy", "gz"))
+    summed = gram_local
+    for over in (("gy", "gz"), "af"):
+        summed = lax.psum(summed, over)
     triangle = jnp.linalg.cholesky(summed)
     basis = basis_init
     for sweep in range(ITERS):

time: 519 us -> 523 us (level)
  the two profiles are of different devices: /device:TPU:23 before, /device:TPU:1 now
where the time goes in v1:
time: 523 us; the launch traced here: 514 us
  waiting for transfers between devices  276 us (53%)
  other arithmetic  171 us (33%)
  blocking collectives  28.8 us (6%)
  between operations  17.5 us (3%)
  matrix products  13.8 us (3%)
  local copies, waits for them, and re-layouts  6.28 us (1%)
    psum x2, waiting for transfers between devices, on_device(): summed = lax.psum(summed, over)  276 us
    another operation x14, other arithmetic, on_device(): triangle = jnp.linalg.cholesky(summed)  78.7 us
    another operation x12, other arithmetic, orthonormal(): factor = jnp.linalg.cholesky(inner_prod)  49.8 us
    another operation x8, other arithmetic, orthonormal(): lax.linalg.triangular_solve(factor, matrix, left_side=False, lower=True,...  42.1 us
    all_to_all x1, blocking collectives, on_device(): lax.all_to_all(arranged, 'af', split_axis=1, concat_axis=0, tiled=True)  28.8 us
  transfers between devices with their start and end apart: 2, of which 2 were waited for; matrix products, arithmetic and copies ran while one was open for 0% of the time, Pallas kernels for 0%

profile of v1, /device:TPU:1, one launch (start us, length us, event | category | flops | bytes accessed | tf_op | source)
XLA Modules:
  0.0 514.2 jit_solution(5079108620588426243)
XLA Ops:
  7.2 0.6 copy-done.5
  7.9 0.1 select_reduce_fusion.8
  8.0 1.1 copy.39
  9.1 0.6 gather_fusion
  9.7 0.1 select_bitcast_fusion
  9.8 28.8 %all_to_all.15 = bf16[32,16,512]{2,0,1:T(8,128)(2,1)S(1)} all-to-all(bf16[32,16,512]{2,0,1:T(8,128)(2,1)S(1)} %select_bitcast_fusion), channel_id=1, replica_groups=mesh['af'=16,'gy'=4,'gz'=8] {'af'}, dimensions={1} | all-to-all | bytes 1048576 | tf_op jit(solution)/shard_map/all_to_all | solution.py:28
  38.6 1.4 convolution_multiply_fusion
  40.1 153.2 %all-reduce.4.cloned.1.call-done = f32[512,512]{0,1:T(8,128)} async-done(((f32[512,512]{0,1:T(8,128)}), f32[512,512]{0,1:T(8,128)}) %all-reduce.4.cloned.1.call-update) | async-done | bytes 1048592 | tf_op jit(solution)/shard_map/psum | solution.py:40
  193.4 123.1 %all-reduce.6.cloned.1.call-done = f32[512,512]{0,1:T(8,128)} async-done(((f32[512,512]{0,1:T(8,128)}), f32[512,512]{0,1:T(8,128)}) %all-reduce.6.cloned.1.call-update) | async-done | bytes 1048592 | tf_op jit(solution)/shard_map/psum | solution.py:40
  316.4 1.6 copy.30
  318.1 0.2 fusion
  318.4 1.0 copy-done.3
  319.3 11.7 %cholesky.120 = f32[128,128]{1,0:T(8,128)S(1)} custom-call(f32[128,128]{1,0:T(8,128)S(1)} %cholesky.382), custom_call_target="Cholesky" | custom-call | tf_op jit(solution)/shard_map/jit(cholesky)/cholesky | solution.py:41
  331.1 9.8 %custom-call.32 = f32[1,128,128]{1,2,0:T(8,128)S(1)} custom-call(f32[1,128,128]{2,1,0:T(8,128)S(1)} %get-tuple-element.26), custom_call_target="InvertDiagBlocksLowerTriangular" | custom-call | tf_op jit(solution)/shard_map/jit(cholesky)/cholesky | solution.py:41
  340.9 0.1 cholesky.251
  341.0 0.3 constant_dynamic-update-slice_fusion.2
  341.4 0.3 convolution_subtract_fusion
  341.7 11.7 %cholesky.244 = f32[128,128]{1,0:T(8,128)S(1)} custom-call(f32[128,128]{1,0:T(8,128)S(1)} %cholesky.386), custom_call_target="Cholesky" | custom-call | tf_op jit(solution)/shard_map/jit(cholesky)/cholesky | solution.py:41
  353.5 10.1 %custom-call.33 = f32[1,128,128]{1,2,0:T(8,128)S(1)} custom-call(f32[1,128,128]{2,1,0:T(8,128)S(1)} %get-tuple-element.23), custom_call_target="InvertDiagBlocksLowerTriangular" | custom-call | tf_op jit(solution)/shard_map/jit(cholesky)/cholesky | solution.py:41
  363.6 0.3 convolution_dynamic-update-slice_fusion
  363.9 0.4 convolution_subtract_fusion.1
  364.3 11.7 %cholesky.265 = f32[128,128]{1,0:T(8,128)S(1)} custom-call(f32[128,128]{1,0:T(8,128)S(1)} %cholesky.391), custom_call_target="Cholesky" | custom-call | tf_op jit(solution)/shard_map/jit(cholesky)/cholesky | solution.py:41
  376.0 0.6 compare_reduce_fusion.5
  376.6 9.8 %custom-call.34 = f32[1,128,128]{1,2,0:T(8,128)S(1)} custom-call(f32[1,128,128]{2,1,0:T(8,128)S(1)} %get-tuple-element.20), custom_call_target="InvertDiagBlocksLowerTriangular" | custom-call | tf_op jit(solution)/shard_map/jit(cholesky)/cholesky | solution.py:41
  386.5 0.2 convolution_dynamic-update-slice_fusion.1
  386.7 0.4 convolution_subtract_fusion.2
  387.1 11.7 %cholesky.282 = f32[128,128]{1,0:T(8,128)S(1)} custom-call(f32[128,128]{1,0:T(8,128)S(1)} %convolution_subtract_fusion.2), custom_call_target="Cholesky" | custom-call | tf_op jit(solution)/shard_map/jit(cholesky)/cholesky | solution.py:41
  398.8 0.7 compare_reduce_fusion.4
  399.5 0.6 compare_reduce_fusion.6
  402.8 0.3 select_select_fusion
  403.1 1.8 fusion.26
  404.9 0.6 fusion.27
  405.5 0.1 copy.31
  405.6 11.7 %cholesky.340 = f32[128,128]{1,0:T(8,128)S(1)} custom-call(f32[128,128]{1,0:T(8,128)S(1)} %fusion.21), custom_call_target="Cholesky" | custom-call | tf_op jit(solution)/shard_map/jit(cholesky)/cholesky | solution.py:12
  417.4 0.6 compare_reduce_fusion.3
  418.0 0.7 fusion.8
  418.7 9.8 %custom-call.38 = f32[1,128,128]{1,2,0:T(8,128)S(1)} custom-call(f32[1,128,128]{2,1,0:T(8,128)S(1)} %fusion.8), custom_call_target="InvertDiagBlocksLowerTriangular" | custom-call | tf_op jit(solution)/shard_map/triangular_solve/custom-call.8 | solution.py:13
  428.5 0.4 convolution_bitcast_fusion.3
  428.9 1.0 fusion.28
  429.9 0.6 fusion.29
  430.5 0.1 copy.32
  430.6 11.9 %cholesky.351 = f32[128,128]{1,0:T(8,128)S(1)} custom-call(f32[128,128]{1,0:T(8,128)S(1)} %fusion.19), custom_call_target="Cholesky" | custom-call | tf_op jit(solution)/shard_map/jit(cholesky)/cholesky | solution.py:12
  442.6 0.6 compare_reduce_fusion.2
  443.2 0.7 fusion.9
  443.9 9.8 %custom-call.39 = f32[1,128,128]{1,2,0:T(8,128)S(1)} custom-call(f32[1,128,128]{2,1,0:T(8,128)S(1)} %fusion.9), custom_call_target="InvertDiagBlocksLowerTriangular" | custom-call | tf_op jit(solution)/shard_map/triangular_solve/custom-call.8 | solution.py:13
  453.7 0.4 convolution_bitcast_fusion.2
  454.1 1.8 fusion.30
  455.9 0.6 fusion.31
  456.5 0.1 copy.33
  456.6 11.7 %cholesky.362 = f32[128,128]{1,0:T(8,128)S(1)} custom-call(f32[128,128]{1,0:T(8,128)S(1)} %fusion.17), custom_call_target="Cholesky" | custom-call | tf_op jit(solution)/shard_map/jit(cholesky)/cholesky | solution.py:12
  468.4 0.6 compare_reduce_fusion.1
  469.0 0.7 fusion.10
  469.7 10.0 %custom-call.40 = f32[1,128,128]{1,2,0:T(8,128)S(1)} custom-call(f32[1,128,128]{2,1,0:T(8,128)S(1)} %fusion.10), custom_call_target="InvertDiagBlocksLowerTriangular" | custom-call | tf_op jit(solution)/shard_map/triangular_solve/custom-call.8 | solution.py:13
  479.7 0.4 convolution_bitcast_fusion.1
  480.2 1.0 fusion.32
  481.2 0.6 fusion.33
  481.8 0.1 copy.34
  481.9 11.7 %cholesky.373 = f32[128,128]{1,0:T(8,128)S(1)} custom-call(f32[128,128]{1,0:T(8,128)S(1)} %fusion.15), custom_call_target="Cholesky" | custom-call | tf_op jit(solution)/shard_map/jit(cholesky)/cholesky | solution.py:12
  493.6 0.6 compare_reduce_fusion
  494.3 0.7 fusion.11
  494.9 9.8 %custom-call.41 = f32[1,128,128]{1,2,0:T(8,128)S(1)} custom-call(f32[1,128,128]{2,1,0:T(8,128)S(1)} %fusion.11), custom_call_target="InvertDiagBlocksLowerTriangular" | custom-call | tf_op jit(solution)/shard_map/triangular_solve/custom-call.8 | solution.py:13
  504.7 0.4 convolution_bitcast_fusion
  505.2 0.9 convolution_convert_fusion
  506.1 0.8 copy.35
  (32 shorter events, 0.5 us)
Async XLA Ops:
  7.2 395.9 %copy-start = (f32[512,128]{1,0:T(8,128)S(1)}, f32[512,128]{1,0:T(8,128)}, u32[]{:S(2)}) copy-start(f32[512,128]{1,0:T(8,128)} %param.8) | copy-start | bytes 786436
  7.2 0.7 copy-start.5
  7.2 186.1 %all-reduce.4.cloned.1.call-start = ((), (), s32[]{:S(2)}) async-start(), calls=%async_computation.1 | async-start | bytes 2097152 | tf_op jit(solution)/shard_map/psum | solution.py:40
  40.1 276.3 %all-reduce.6.cloned.1.call-start = ((), (), s32[]{:S(2)}) async-start(), calls=%async_computation.2 | async-start | bytes 2097152 | tf_op jit(solution)/shard_map/psum | solution.py:40
  316.4 1.7 copy-start.2
  318.3 1.0 copy-start.3
  319.3 21.7 %copy-start.4 = (f32[512,512]{1,0:T(8,128)S(1)}, f32[512,512]{1,0:T(8,128)}, u32[]{:S(2)}) copy-start(f32[512,512]{1,0:T(8,128)} %copy-done.3) | copy-start | bytes 3145732
  403.1 77.1 %copy-start.1 = (f32[512,512]{1,0:T(8,128)}, f32[512,512]{1,0:T(8,128)S(1)}, u32[]{:S(2)}) copy-start(f32[512,512]{1,0:T(8,128)S(1)} %select_select_fusion) | copy-start | bytes 3145732
Sparse Core Ops, SparseCore 0:
  40.2 153.0 all-reduce.3
  195.7 120.7 all-reduce.5
